TPU v7x, 1024 devices: a whole 4x4x32 slice. The times are simulated.
1024 devices in a mesh: dp: 16 (over y, x_lo, core), seq: 64 (over x_hi, z).
Axes of the slice: x: 4 (x_hi: 2, x_lo: 2; x = x_hi * 2 + x_lo), y: 4, z: 32, core: 2. Of those that a mesh axis runs over, the one named last changes fastest.
Arguments:
- grad_out: bfloat16 [16, 8192, 4096], P('dp', 'seq'), may hold values from -6 to 6
- block_in: bfloat16 [16, 8192, 4096], P('dp', 'seq'), may hold values from -0.0234375 to 0.0234375
- residues: float32 [8, 4096], replicated, may hold values from -2 to 2
- decay_rates: float32 [8], replicated
Outputs:
- grad_in: bfloat16 [16, 8192, 4096], P('dp', 'seq')
- residue_grad: float32 [8, 4096], P(None, 'dp')
All inputs are finite; a program needn't handle non-finite values.
Results may differ from a plain program's by a relative error of at most 0.0068.
Values sent between devices are 32-bit elements; how exact they have to be, the bound alone decides.
A program may use at most 64 MiB of HBM per device.

v0:
```python
import jax
import jax.numpy as jnp
from jax import lax
from jax.sharding import PartitionSpec as P


def prefix(shard, axis, combine, identity):
    count, index = (lax.axis_size(axis), lax.axis_index(axis))
    everything = jax.tree.map(lambda part: lax.all_gather(part, axis), shard)
    start = jax.tree.map(
        lambda part, zero: jnp.broadcast_to(jnp.asarray(zero, part.dtype), part.shape),
        shard,
        identity,
    )

    def step(k, before):
        at = count - 1 - k
        reached = at > index
        new = combine(before, jax.tree.map(lambda part: part[at], everything))
        return jax.tree.map(lambda a, b: jnp.where(reached, a, b), new, before)

    return lax.fori_loop(0, count, step, start)


def modal_tables(decay_rates, block_rows):
    offsets = jnp.arange(block_rows, dtype=jnp.float32)
    mode_gain = jnp.sqrt(1.0 - jnp.exp(-2.0 * decay_rates))
    lag_steps = offsets[None, :] - offsets[:, None]
    decay_table = jnp.where(
        lag_steps[None] >= 0,
        mode_gain[:, None, None]
        * jnp.exp(-decay_rates[:, None, None] * jnp.maximum(lag_steps[None], 0.0)),
        0.0,
    ).astype(jnp.bfloat16)
    carry_table = (
        mode_gain[None, :] * jnp.exp(-decay_rates[None, :] * (block_rows - offsets[:, None]))
    ).astype(jnp.bfloat16)
    state_table = jnp.exp(-decay_rates[:, None] * offsets[None, :]).astype(jnp.bfloat16)
    block_decay = jnp.exp(-decay_rates * block_rows)
    return (decay_table, carry_table, state_table, block_decay)


def local_terms(grad_out, block_in, residues, decay_table, carry_table, state_table):
    batch_rows, block_rows, channel_count = grad_out.shape
    mode_count = residues.shape[0]
    stacked_table = jnp.transpose(decay_table, (1, 0, 2)).reshape(
        block_rows, mode_count * block_rows
    )
    scaled = (
        (grad_out[:, None, :, :] * residues[None, :, None, :])
        .astype(jnp.bfloat16)
        .reshape(batch_rows, mode_count * block_rows, channel_count)
    )
    local_grad = jnp.einsum(
        "sk,bkc->bsc", stacked_table, scaled, preferred_element_type=jnp.float32
    )
    block_state = jnp.einsum(
        "rt,btc->brc", state_table, grad_out, preferred_element_type=jnp.float32
    )
    pieces = []
    for mode_index in range(mode_count):
        weighted = jnp.einsum(
            "st,bsc->btc", decay_table[mode_index], block_in, preferred_element_type=jnp.float32
        )
        pieces.append(jnp.sum(weighted * grad_out, axis=(0, 1)))
    local_part = jnp.stack(pieces)
    carry_weights = jnp.einsum(
        "sr,bsc->brc", carry_table, block_in, preferred_element_type=jnp.float32
    )
    return (local_grad, block_state, local_part, carry_weights)


def local(grad_out, block_in, residues, decay_rates):
    batch_rows, block_rows, channel_count = grad_out.shape
    decay_table, carry_table, state_table, block_decay = modal_tables(decay_rates, block_rows)
    local_grad, block_state, local_part, carry_weights = local_terms(
        grad_out, block_in, residues, decay_table, carry_table, state_table
    )
    decay_stack = block_decay[None, :, None]

    def combine(earlier_part, later_part):
        return (later_part[0] * earlier_part[0], later_part[1] + later_part[0] * earlier_part[1])

    identity = (jnp.ones_like(decay_stack), jnp.zeros_like(block_state))
    incoming = prefix((decay_stack, block_state), "seq", combine, identity)[1]
    carried = jnp.einsum(
        "sr,brc->bsc",
        carry_table.astype(jnp.float32),
        residues[None] * incoming,
        precision=lax.Precision.HIGHEST,
    )
    grad_in = (local_grad + carried).astype(jnp.bfloat16)
    partial_value = local_part + jnp.sum(incoming * carry_weights, axis=0)
    whole_sum = lax.psum(partial_value, "seq")
    residue_grad = lax.psum_scatter(whole_sum, "dp", scatter_dimension=1, tiled=True)
    return (grad_in, residue_grad)


def solution(mesh):
    placed = (P("dp", "seq", None), P("dp", "seq", None), P(), P())
    return jax.shard_map(
        local,
        mesh=mesh,
        in_specs=placed,
        out_specs=(P("dp", "seq", None), P(None, "dp")),
        check_vma=False,
    )
```

profile of v0, /device:TPU:4, one launch (start us, length us, event | category | flops | bytes accessed | tf_op | source)
XLA Modules:
  0.0 674.5 jit_solution(17559665584942331709)
XLA Ops:
  7.2 1.4 dynamic-slice
  10.1 2.2 convolution_bitcast_fusion.9
  12.4 159.4 %all-reduce = f32[512]{0:T(512)S(1)} all-reduce(f32[512]{0:T(512)S(1)} %get-tuple-element.184), channel_id=3, replica_groups=mesh['dp'=16,'seq'=64] {'seq'}, use_global_device_ids=true, to_apply=%add | all-reduce | flops 512 | bytes 4096
  172.4 1.5 bitcast_convert_fusion
  173.9 3.0 copy.13
  180.1 1.1 fusion.12
  181.2 1.1 fusion.11
  182.3 1.1 fusion.10
  183.3 1.1 stack.35
  184.5 154.9 %all-gather.4.cloned.1.call-done = f32[64,8,4096]{2,1,0:T(8,128)} async-done(((f32[1,8,4096]{2,1,0:T(8,128)}), f32[64,8,4096]{2,1,0:T(8,128)}) %all-gather.4.cloned.1.call-update) | async-done | bytes 8388624 | tf_op jit(solution)/shard_map/all_gather | solution.py:9
  339.4 106.2 %while.16 = (s32[]{:T(128)}, f32[1,8,4096]{2,1,0:T(8,128)S(1)}, s32[]{:T(128)}, f32[64,1,8,4096]{3,2,1,0:T(8,128)}, f32[64,1,8,1]{2,3,1,0:T(1,128)}, /*index=5*/s32[]{:T(128)}, s32[]{:T(128)}, s32[]{:T(128)}, s32[]{:T(128)}) while((s32[]{:T(128)}, f32[1,8,4096]{2,1,0:T(8,128)S(1)}, s32[]{:T(128)}, f32[64,1,8,4096]{3,2,1,0:T(8,128)}, ...), condition=%wide.region_1.2_spmd.clone, body=%wide.region_0.1_spmd.clone.sunk | while | flops 131080 | bytes 393487 | solution.py:22
  343.3 1.0 fusion.45
  346.7 1.0 fusion.45
  350.0 1.0 fusion.45
  351.6 1.0 fusion.45
  358.3 1.0 fusion.45
  361.6 1.0 fusion.45
  371.5 1.0 fusion.45
  374.8 1.0 fusion.45
  379.8 1.0 fusion.45
  383.1 1.0 fusion.45
  384.8 1.0 fusion.45
  386.4 1.0 fusion.45
  391.5 1.0 fusion.45
  393.2 1.0 fusion.45
  394.8 1.0 fusion.45
  445.6 1.7 fusion.9
  447.4 5.5 fusion.4
  452.9 1.9 fusion.6
  454.8 1.3 copy.16
  456.1 60.2 %reduce-scatter.2.cloned.1.call-done = f32[8,256]{1,0:T(8,128)} async-done(((f32[8,4096]{1,0:T(8,128)}), f32[8,256]{1,0:T(8,128)}) %reduce-scatter.2.cloned.1.call-update) | async-done | bytes 8208 | tf_op jit(solution)/shard_map/reduce_scatter | solution.py:95
  516.3 151.4 %psum.8 = f32[8,256]{1,0:T(8,128)} all-reduce(f32[8,256]{1,0:T(8,128)} %reduce-scatter.2.cloned.1.call-done), channel_id=1, replica_groups=mesh['dp'=16,'seq'=64] {'seq'}, use_global_device_ids=true, to_apply=%region_10.11 | all-reduce | flops 2048 | bytes 16384 | tf_op jit(solution)/shard_map/psum | solution.py:94
  (150 shorter events, 94.1 us)
Async XLA Ops:
  7.2 170.5 %copy-start = (bf16[1,128,4096]{2,1,0:T(8,128)(2,1)S(1)}, bf16[1,128,4096]{2,1,0:T(8,128)(2,1)}, u32[]{:S(2)}) copy-start(bf16[1,128,4096]{2,1,0:T(8,128)(2,1)} %param.7) | copy-start | bytes 3145732
  7.2 165.2 %copy-start.1 = (bf16[1,128,4096]{2,1,0:T(8,128)(2,1)S(1)}, bf16[1,128,4096]{2,1,0:T(8,128)(2,1)}, u32[]{:S(2)}) copy-start(bf16[1,128,4096]{2,1,0:T(8,128)(2,1)} %param.6) | copy-start | bytes 3145732
  7.2 332.2 %all-gather.4.cloned.1.call-start = ((), (), s32[]{:S(2)}) async-start(), calls=%async_computation.1 | async-start | bytes 8519680 | tf_op jit(solution)/shard_map/all_gather | solution.py:9
  10.1 166.9 %copy-start.6 = (f32[8]{0:T(128)}, f32[8]{0:T(128)S(1)}, u32[]{:S(2)}) copy-start(f32[8]{0:T(128)S(1)} %get-tuple-element.185) | copy-start | bytes 100
  10.1 166.9 %copy-start.8 = (f32[8]{0:T(128)}, f32[8]{0:T(128)S(1)}, u32[]{:S(2)}) copy-start(f32[8]{0:T(128)S(1)} %get-tuple-element.186) | copy-start | bytes 100
  12.3 504.0 %reduce-scatter.2.cloned.1.call-start = ((), (), s32[]{:S(2)}) async-start(), calls=%async_computation.2 | async-start | bytes 139264 | tf_op jit(solution)/shard_map/reduce_scatter | solution.py:95
  176.9 0.6 copy-start.4
  183.3 264.0 %copy-start.2 = (f32[128,4096]{0,1:T(8,128)S(1)}, f32[128,4096]{0,1:T(8,128)}, u32[]{:S(2)}) copy-start(f32[128,4096]{0,1:T(8,128)} %copy.13) | copy-start | bytes 6291460
  184.4 262.9 %copy-start.5 = (pred[128,128]{1,0:T(8,128)(4,1)S(1)}, pred[128,128]{1,0:T(8,128)(4,1)}, u32[]{:S(2)}) copy-start(pred[128,128]{1,0:T(8,128)(4,1)} %copy-done.4) | copy-start | bytes 49156
  184.4 262.9 %copy-start.7 = (f32[8]{0:T(128)S(1)}, f32[8]{0:T(128)}, u32[]{:S(2)}) copy-start(f32[8]{0:T(128)} %copy-done.6) | copy-start | bytes 100
  184.5 262.9 %copy-start.9 = (f32[8]{0:T(128)S(1)}, f32[8]{0:T(128)}, u32[]{:S(2)}) copy-start(f32[8]{0:T(128)} %copy-done.8) | copy-start | bytes 100
  447.3 5.6 copy-start.3
Sparse Core Ops, SparseCore 0:
  12.9 326.4 all-gather.3
  447.4 68.8 reduce-scatter.1
where the time goes:
time: 677 us; the launch traced here: 675 us
  blocking collectives  311 us (46%)
  waiting for transfers between devices  215 us (32%)
  other arithmetic  65.8 us (10%)
  local copies, waits for them, and re-layouts  49 us (7%)
  matrix products  16.9 us (2%)
  between operations  14.9 us (2%)
    unnamed x1, blocking collectives  159 us
    all_gather x1, waiting for transfers between devices, prefix(): everything = jax.tree.map(lambda part: lax.all_gather(part, axis), shard)  155 us
    psum x1, blocking collectives, local(): whole_sum = lax.psum(partial_value, 'seq')  151 us
    select_n x64, other arithmetic, step(): return jax.tree.map(lambda a, b: jnp.where(reached, a, b), new, before)  63.3 us
    reduce_scatter x1, waiting for transfers between devices, local(): lax.psum_scatter(whole_sum, 'dp', scatter_dimension=1, tiled=True)  60.2 us
    mul x64, local copies, waits for them, and re-layouts, combine(): later_part[0] * earlier_part[1]  40.9 us
  transfers between devices with their start and end apart: 2, of which 2 were waited for; matrix products, arithmetic and copies ran while one was open for 3% of the time, Pallas kernels for 0%

commit v1 on v0

v1 whole, which is shorter than its diff:
```python
import functools

import jax
import jax.numpy as jnp
from jax import lax
from jax.experimental import pallas as pl
from jax.experimental.pallas import tpu as pltpu
from jax.sharding import PartitionSpec as P

MESH = pl.DeviceIdType.MESH
F32 = jnp.float32
BF16 = jnp.bfloat16


def kernel(
    tiles, rates, g_hbm, x_hbm, res_hbm, gin_ref, rgrad_ref,
    g, x, res, dt, lg, s_out, w_out, l_out, s_in, w_in, l_in, inc_out, inc_in,
    tw_out, tw_in, x_out, x_in, lsum, lz_in, lr_out, lr_in, r_out, r_in,
    in_sem, snd, rcv, r_rcv,
):
    modes, rows = 8, 128
    d = lax.axis_index("dp")
    seq = lax.axis_index("seq")
    h, z = lax.div(seq, tiles), lax.rem(seq, tiles)
    p = 2 * d + h
    owner = lax.div(z, 2) == d

    def wrap(v):
        return lax.rem(v + tiles, tiles)

    def line(zz):
        return (d, h * tiles + zz)

    def plane(pp):
        return (lax.div(pp, 2), lax.rem(pp, 2) * tiles + z)

    def send(kind, src, dst, dev):
        pltpu.make_async_remote_copy(
            src_ref=src, dst_ref=dst, send_sem=snd.at[kind], recv_sem=rcv.at[kind],
            device_id=dev, device_id_type=MESH,
        ).start()

    def wait_tiles(buf, sem, lo, n):
        part = buf.at[pl.ds(lo, n)]
        pltpu.make_async_copy(part, part, sem).wait()

    copy_g = pltpu.make_async_copy(g_hbm.at[0], g, in_sem.at[0])
    copy_x = pltpu.make_async_copy(x_hbm.at[0], x, in_sem.at[1])
    copy_r = pltpu.make_async_copy(res_hbm, res, in_sem.at[2])
    copy_g.start()
    copy_x.start()
    copy_r.start()

    barrier = pltpu.get_barrier_semaphore()

    def greet(j, c):
        pl.semaphore_signal(barrier, inc=1, device_id=line(wrap(z + j)), device_id_type=MESH)
        pl.semaphore_signal(barrier, inc=1, device_id=plane(wrap(p + j)), device_id_type=MESH)
        return c

    lax.fori_loop(1, tiles, greet, 0)

    mode_row = lax.broadcasted_iota(jnp.int32, (modes, 128), 0)
    rate = jnp.zeros((modes, 128), F32)
    for r in range(modes):
        rate = jnp.where(mode_row == r, rates[r], rate)
    gain = jnp.sqrt(1.0 - jnp.exp(-2.0 * rate))
    pos = lax.broadcasted_iota(jnp.int32, (modes, 128), 1).astype(F32)
    state_table = jnp.exp(-rate * pos).astype(BF16)
    carry_t = (gain * jnp.exp(-rate * (rows - pos))).astype(BF16)
    decay = jnp.exp(-rate * float(rows))
    lag = (
        lax.broadcasted_iota(jnp.int32, (rows, rows), 1)
        - lax.broadcasted_iota(jnp.int32, (rows, rows), 0)
    ).astype(F32)
    causal = lag >= 0
    lag = jnp.maximum(lag, 0.0)
    for r in range(modes):
        full = jnp.full((rows, rows), rates[r], F32)
        gain_r = jnp.sqrt(1.0 - jnp.exp(-2.0 * full))
        dt[r] = jnp.where(causal, gain_r * jnp.exp(-full * lag), 0.0).astype(BF16)
    col = lax.rem(lax.broadcasted_iota(jnp.int32, (rows, 32), 1), modes)
    part = lax.div(lax.broadcasted_iota(jnp.int32, (rows, 32), 1), modes)
    at = lax.broadcasted_iota(jnp.int32, (rows, 32), 0).astype(F32)
    rate_c = jnp.zeros((rows, 32), F32)
    for r in range(modes):
        rate_c = jnp.where(col == r, rates[r], rate_c)
    gain_c = jnp.sqrt(1.0 - jnp.exp(-2.0 * rate_c))
    carry3 = jnp.where(part < 3, gain_c * jnp.exp(-rate_c * (rows - at)), 0.0).astype(BF16)

    copy_g.wait()
    copy_x.wait()
    copy_r.wait()

    def states(i, c):
        cols = pl.ds(pl.multiple_of(i * 256, 256), 256)
        s = jnp.dot(state_table, g[:, cols], preferred_element_type=F32)
        w = jnp.dot(carry_t, x[:, cols], preferred_element_type=F32)
        for t in range(2):
            s_out[2 * i + t] = s[:, t * 128:(t + 1) * 128]
            w_out[2 * i + t] = w[:, t * 128:(t + 1) * 128]
        return c

    lax.fori_loop(0, tiles // 2, states, 0)

    def local(i, c):
        cols = pl.ds(pl.multiple_of(i * 256, 256), 256)
        gc = g[:, cols]
        xc = x[:, cols].astype(F32)
        total = jnp.zeros((rows, 256), F32)
        sums = []
        for r in range(modes):
            v = jnp.dot(dt[r], gc, preferred_element_type=F32)
            total = total + v * res[r:r + 1, cols]
            sums.append(jnp.sum(v * xc, axis=0, keepdims=True))
        lg[:, cols] = total
        lp = jnp.concatenate(sums, axis=0)
        for t in range(2):
            l_out[2 * i + t] = lp[:, t * 128:(t + 1) * 128]
        return c

    lax.fori_loop(0, tiles // 2, local, 0)

    pl.semaphore_wait(barrier, 2 * (tiles - 1))

    S, W, LP, INC, TW, X, LZ, LR, R = range(9)

    def send_s(j, c):
        to = wrap(z + j)
        send(S, s_out.at[to], s_in.at[tiles - j], line(to))
        return c

    def send_w(j, c):
        to = wrap(z + j)
        send(W, w_out.at[to], w_in.at[tiles - j], line(to))
        return c

    def send_l(j, c):
        to = wrap(p + j)
        send(LP, l_out.at[to], l_in.at[tiles - j], plane(to))
        return c

    lax.fori_loop(1, tiles, send_s, 0)
    lax.fori_loop(1, tiles, send_w, 0)
    lax.fori_loop(1, tiles, send_l, 0)
    s_in[0] = s_out[z]
    w_in[0] = w_out[z]

    wait_tiles(l_in, rcv.at[LP], 1, tiles - 1)
    lsum[0] = l_out[p] + jnp.sum(l_in[1:tiles], axis=0)

    @pl.when(z != p)
    def _():
        send(LZ, lsum.at[0], lz_in.at[wrap(z - p)], line(p))

    wait_tiles(s_in, rcv.at[S], 1, tiles - 1)

    def scan(keep):
        def step(i, carry):
            slot = wrap(tiles - 1 - i - z)
            if keep:
                inc_out[slot] = carry
            return s_in[slot] + decay * carry
        return step

    tw_out[0] = lax.fori_loop(0, tiles, scan(False), jnp.zeros((modes, 128), F32), unroll=4)
    twin = plane(p + 1 - 2 * h)
    send(TW, tw_out.at[0], tw_in.at[0], twin)
    wait_tiles(tw_in, rcv.at[TW], 0, 1)
    start = jnp.where(h == 0, tw_in[0], 0.0)
    lax.fori_loop(0, tiles, scan(True), start, unroll=4)

    def send_inc(j, c):
        send(INC, inc_out.at[j], inc_in.at[tiles - j], line(wrap(z + j)))
        return c

    lax.fori_loop(1, tiles, send_inc, 0)
    inc_in[0] = inc_out[0]

    wait_tiles(w_in, rcv.at[W], 1, tiles - 1)
    cross = jnp.sum(inc_out[...] * w_in[...], axis=0)
    x_out[0] = cross
    to_d = 2 * lax.div(z, 2)
    for half in range(2):
        to = to_d + half

        @pl.when(to != p)
        def _(to=to):
            send(X, x_out.at[0], x_in.at[wrap(p - to)], plane(to))

    @pl.when(owner)
    def _():
        @pl.when(z == p)
        def _():
            wait_tiles(lz_in, rcv.at[LZ], 1, tiles - 1)
            lr_out[0] = lsum[0] + jnp.sum(lz_in[1:tiles], axis=0)
            send(LR, lr_out.at[0], lr_in.at[0], twin)

        @pl.when(z != p)
        def _():
            wait_tiles(lr_in, rcv.at[LR], 0, 1)
            lr_out[0] = lr_in[0]

        wait_tiles(x_in, rcv.at[X], 1, tiles - 1)
        r_out[0] = lr_out[0] + x_out[0] + jnp.sum(x_in[1:tiles], axis=0)

        def send_r(j, c):
            to = wrap(z + j)
            pltpu.make_async_remote_copy(
                src_ref=r_out.at[0], dst_ref=r_in.at[lax.rem(z, 2)],
                send_sem=snd.at[R], recv_sem=r_rcv.at[lax.rem(z, 2)],
                device_id=line(to), device_id_type=MESH,
            ).start()
            return c

        lax.fori_loop(1, tiles, send_r, 0)

    wait_tiles(inc_in, rcv.at[INC], 1, tiles - 1)

    def finish(i, c):
        cols = pl.ds(pl.multiple_of(i * 256, 256), 256)
        inc = jnp.concatenate([inc_in[wrap(2 * i - z)], inc_in[wrap(2 * i + 1 - z)]], axis=1)
        u = inc * res[:, cols]
        u0 = u.astype(BF16).astype(F32)
        u1 = (u - u0).astype(BF16).astype(F32)
        u2 = u - u0 - u1
        u3 = jnp.concatenate([u0, u1, u2, jnp.zeros_like(u)], axis=0).astype(BF16)
        out = lg[:, cols] + jnp.dot(carry3, u3, preferred_element_type=F32)
        gin_ref[0, :, cols] = out.astype(BF16)
        return c

    lax.fori_loop(0, tiles // 2, finish, 0)

    for i in range(2):
        mine = 2 * d + i == z

        @pl.when(jnp.logical_not(mine))
        def _(i=i):
            wait_tiles(r_in, r_rcv.at[i], i, 1)
            rgrad_ref[:, i * 128:(i + 1) * 128] = r_in[i]

        @pl.when(mine)
        def _(i=i):
            rgrad_ref[:, i * 128:(i + 1) * 128] = r_out[0]

    for kind, buf in ((S, s_in), (W, w_in), (LP, l_in), (INC, inc_in)):
        wait_tiles(buf, snd.at[kind], 1, tiles - 1)
    wait_tiles(tw_in, snd.at[TW], 0, 1)

    @pl.when(z != p)
    def _():
        wait_tiles(lsum, snd.at[LZ], 0, 1)

    for half in range(2):
        @pl.when(to_d + half != p)
        def _():
            wait_tiles(x_out, snd.at[X], 0, 1)

    @pl.when(owner)
    def _():
        wait_tiles(s_in, snd.at[R], 1, tiles - 1)

        @pl.when(z == p)
        def _():
            wait_tiles(lr_out, snd.at[LR], 0, 1)


def local(grad_out, block_in, residues, decay_rates):
    _, rows, channels = grad_out.shape
    tiles = channels // 128
    modes = residues.shape[0]
    vm = pltpu.VMEM
    many = vm((tiles, modes, 128), F32)
    one = vm((1, modes, 128), F32)
    anywhere = pl.BlockSpec(memory_space=pl.ANY)
    return pl.pallas_call(
        functools.partial(kernel, tiles),
        out_shape=(
            jax.ShapeDtypeStruct((1, rows, channels), BF16),
            jax.ShapeDtypeStruct((modes, 256), F32),
        ),
        in_specs=[pl.BlockSpec(memory_space=pltpu.SMEM), anywhere, anywhere, anywhere],
        out_specs=(pl.BlockSpec(memory_space=pltpu.VMEM), pl.BlockSpec(memory_space=pltpu.VMEM)),
        scratch_shapes=[
            vm((rows, channels), BF16),
            vm((rows, channels), BF16),
            vm((modes, channels), F32),
            vm((modes, rows, rows), BF16),
            vm((rows, channels), F32),
            many, many, many, many, many, many, many, many,
            one, one, one, many, one, many, one, one, one, vm((2, modes, 128), F32),
            pltpu.SemaphoreType.DMA((3,)),
            pltpu.SemaphoreType.DMA((9,)),
            pltpu.SemaphoreType.DMA((9,)),
            pltpu.SemaphoreType.DMA((2,)),
        ],
        compiler_params=pltpu.CompilerParams(collective_id=0, has_side_effects=True),
        name="modal_backward",
    )(decay_rates, grad_out, block_in, residues)


def solution(mesh):
    placed = (P("dp", "seq", None), P("dp", "seq", None), P(), P())
    return jax.shard_map(
        local,
        mesh=mesh,
        in_specs=placed,
        out_specs=(P("dp", "seq", None), P(None, "dp")),
        check_vma=False,
    )
```

time: 677 us -> 88.1 us (0.13)
  the two profiles are of different devices: /device:TPU:4 before, /device:TPU:16 now
where the time goes in v1:
time: 88.1 us; the launch traced here: 87.9 us
  Pallas kernels  84.4 us (96%)
  local copies, waits for them, and re-layouts  2.9 us (3%)
    pallas_call x1, Pallas kernels, local(): pl.pallas_call(functools.partial(kernel, tiles), out_shape=(jax.ShapeDtyp...  84.4 us
    unnamed x4, local copies, waits for them, and re-layouts  2.9 us

profile of v1, /device:TPU:16, one launch (start us, length us, event | category | flops | bytes accessed | tf_op | source)
XLA Modules:
  0.0 87.9 jit_solution(17339794762561495043)
XLA Ops:
  0.6 84.4 %modal_backward.1 = (bf16[1,128,4096]{2,1,0:T(8,128)(2,1)}, f32[8,256]{1,0:T(8,128)}) custom-call(f32[8]{0:T(128)} %rates.1, bf16[1,128,4096]{2,1,0:T(8,128)(2,1)} %g_hbm.1, bf16[1,128,4096]{2,1,0:T(8,128)(2,1)} %x_hbm.1, f32[8,4096]{1,0:T(8,128)} %res_hbm.1), custom_call_target="tpu_custom_call" | custom-call | tf_op jit(solution)/shard_map/modal_backward/pallas_call | solution.py:276
  85.0 0.0 copy-start
  85.0 2.3 %copy.8 = bf16[1,128,4096]{2,1,0:T(8,128)(2,1)} copy(bf16[1,128,4096]{2,1,0:T(8,128)(2,1)} %get-tuple-element.4) | data formatting | bytes 2097152
  87.3 0.0 copy-done
  87.3 0.6 copy.9
Async XLA Ops:
  85.0 2.3 %copy-start = (f32[8,256]{1,0:T(8,128)S(1)}, f32[8,256]{1,0:T(8,128)}, u32[]{:S(2)}) copy-start(f32[8,256]{1,0:T(8,128)} %get-tuple-element.5) | copy-start | bytes 24580

commit v2 on v1

--- a/solution.py
+++ b/solution.py
@@ -15,7 +15,7 @@
 def kernel(
     tiles, rates, g_hbm, x_hbm, res_hbm, gin_ref, rgrad_ref,
     g, x, res, dt, lg, s_out, w_out, l_out, s_in, w_in, l_in, inc_out, inc_in,
-    tw_out, tw_in, x_out, x_in, lsum, lz_in, lr_out, lr_in, r_out, r_in,
+    tw_out, tw_in, x_out, x_in, lsum, lz_in, r_out, r_in,
     in_sem, snd, rcv, r_rcv,
 ):
     modes, rows = 8, 128
@@ -53,12 +53,22 @@
 
     barrier = pltpu.get_barrier_semaphore()
 
-    def greet(j, c):
-        pl.semaphore_signal(barrier, inc=1, device_id=line(wrap(z + j)), device_id_type=MESH)
-        pl.semaphore_signal(barrier, inc=1, device_id=plane(wrap(p + j)), device_id_type=MESH)
-        return c
-
-    lax.fori_loop(1, tiles, greet, 0)
+    def offset(i):
+        m = lax.div(i, 2)
+        return tiles // 2 + jnp.where(lax.rem(i, 2) == 0, m, -m)
+
+    def greet_line(i, c):
+        to = line(wrap(z + offset(i)))
+        pl.semaphore_signal(barrier, inc=1, device_id=to, device_id_type=MESH)
+        return c
+
+    def greet_plane(j, c):
+        to = plane(wrap(p + j))
+        pl.semaphore_signal(barrier, inc=1, device_id=to, device_id_type=MESH)
+        return c
+
+    lax.fori_loop(1, tiles, greet_line, 0)
+    lax.fori_loop(1, tiles, greet_plane, 0)
 
     mode_row = lax.broadcasted_iota(jnp.int32, (modes, 128), 0)
     rate = jnp.zeros((modes, 128), F32)
@@ -123,35 +133,40 @@
 
     pl.semaphore_wait(barrier, 2 * (tiles - 1))
 
-    S, W, LP, INC, TW, X, LZ, LR, R = range(9)
-
-    def send_s(j, c):
+    S, W, LP, INC, TW, X, LZ, R = range(8)
+
+    def send_s(i, c):
+        j = offset(i)
         to = wrap(z + j)
         send(S, s_out.at[to], s_in.at[tiles - j], line(to))
         return c
 
-    def send_w(j, c):
+    def send_w(i, c):
+        j = offset(i)
         to = wrap(z + j)
         send(W, w_out.at[to], w_in.at[tiles - j], line(to))
         return c
 
     def send_l(j, c):
         to = wrap(p + j)
-        send(LP, l_out.at[to], l_in.at[tiles - j], plane(to))
-        return c
-
+        pair = pl.ds(2 * lax.div(to, 2), 2)
+        send(LP, l_out.at[pair], l_in.at[tiles - j], plane(to))
+        return c
+
+    lax.fori_loop(1, tiles, send_l, 0)
     lax.fori_loop(1, tiles, send_s, 0)
-    lax.fori_loop(1, tiles, send_w, 0)
-    lax.fori_loop(1, tiles, send_l, 0)
     s_in[0] = s_out[z]
     w_in[0] = w_out[z]
 
     wait_tiles(l_in, rcv.at[LP], 1, tiles - 1)
-    lsum[0] = l_out[p] + jnp.sum(l_in[1:tiles], axis=0)
-
-    @pl.when(z != p)
-    def _():
-        send(LZ, lsum.at[0], lz_in.at[wrap(z - p)], line(p))
+    lsum[...] = l_out[pl.ds(2 * d, 2)] + jnp.sum(l_in[1:tiles], axis=0)
+    for i in range(2):
+        @pl.when(2 * d + i != z)
+        def _(i=i):
+            to = 2 * d + i
+            send(LZ, lsum.at[i], lz_in.at[wrap(z - to)], line(to))
+
+    lax.fori_loop(1, tiles, send_w, 0)
 
     wait_tiles(s_in, rcv.at[S], 1, tiles - 1)
 
@@ -170,7 +185,8 @@
     start = jnp.where(h == 0, tw_in[0], 0.0)
     lax.fori_loop(0, tiles, scan(True), start, unroll=4)
 
-    def send_inc(j, c):
+    def send_inc(i, c):
+        j = offset(i)
         send(INC, inc_out.at[j], inc_in.at[tiles - j], line(wrap(z + j)))
         return c
 
@@ -190,22 +206,15 @@
 
     @pl.when(owner)
     def _():
-        @pl.when(z == p)
-        def _():
-            wait_tiles(lz_in, rcv.at[LZ], 1, tiles - 1)
-            lr_out[0] = lsum[0] + jnp.sum(lz_in[1:tiles], axis=0)
-            send(LR, lr_out.at[0], lr_in.at[0], twin)
-
-        @pl.when(z != p)
-        def _():
-            wait_tiles(lr_in, rcv.at[LR], 0, 1)
-            lr_out[0] = lr_in[0]
-
+        wait_tiles(lz_in, rcv.at[LZ], 1, tiles - 1)
         wait_tiles(x_in, rcv.at[X], 1, tiles - 1)
-        r_out[0] = lr_out[0] + x_out[0] + jnp.sum(x_in[1:tiles], axis=0)
-
-        def send_r(j, c):
-            to = wrap(z + j)
+        r_out[0] = (
+            lsum[lax.rem(z, 2)] + jnp.sum(lz_in[1:tiles], axis=0)
+            + x_out[0] + jnp.sum(x_in[1:tiles], axis=0)
+        )
+
+        def send_r(i, c):
+            to = wrap(z + offset(i))
             pltpu.make_async_remote_copy(
                 src_ref=r_out.at[0], dst_ref=r_in.at[lax.rem(z, 2)],
                 send_sem=snd.at[R], recv_sem=r_rcv.at[lax.rem(z, 2)],
@@ -247,9 +256,10 @@
         wait_tiles(buf, snd.at[kind], 1, tiles - 1)
     wait_tiles(tw_in, snd.at[TW], 0, 1)
 
-    @pl.when(z != p)
-    def _():
-        wait_tiles(lsum, snd.at[LZ], 0, 1)
+    for i in range(2):
+        @pl.when(2 * d + i != z)
+        def _():
+            wait_tiles(lsum, snd.at[LZ], 0, 1)
 
     for half in range(2):
         @pl.when(to_d + half != p)
@@ -259,10 +269,6 @@
     @pl.when(owner)
     def _():
         wait_tiles(s_in, snd.at[R], 1, tiles - 1)
-
-        @pl.when(z == p)
-        def _():
-            wait_tiles(lr_out, snd.at[LR], 0, 1)
 
 
 def local(grad_out, block_in, residues, decay_rates):
@@ -272,13 +278,15 @@
     vm = pltpu.VMEM
     many = vm((tiles, modes, 128), F32)
     one = vm((1, modes, 128), F32)
+    pair = vm((2, modes, 128), F32)
     anywhere = pl.BlockSpec(memory_space=pl.ANY)
+    shapes = (
+        jax.ShapeDtypeStruct((1, rows, channels), BF16),
+        jax.ShapeDtypeStruct((modes, 256), F32),
+    )
     return pl.pallas_call(
         functools.partial(kernel, tiles),
-        out_shape=(
-            jax.ShapeDtypeStruct((1, rows, channels), BF16),
-            jax.ShapeDtypeStruct((modes, 256), F32),
-        ),
+        out_shape=tuple(vm(a.shape, a.dtype) for a in shapes),
         in_specs=[pl.BlockSpec(memory_space=pltpu.SMEM), anywhere, anywhere, anywhere],
         out_specs=(pl.BlockSpec(memory_space=pltpu.VMEM), pl.BlockSpec(memory_space=pltpu.VMEM)),
         scratch_shapes=[
@@ -287,11 +295,12 @@
             vm((modes, channels), F32),
             vm((modes, rows, rows), BF16),
             vm((rows, channels), F32),
-            many, many, many, many, many, many, many, many,
-            one, one, one, many, one, many, one, one, one, vm((2, modes, 128), F32),
+            many, many, many, many, many,
+            vm((tiles, 2, modes, 128), F32), many, many,
+            one, one, one, many, pair, many, one, pair,
             pltpu.SemaphoreType.DMA((3,)),
-            pltpu.SemaphoreType.DMA((9,)),
-            pltpu.SemaphoreType.DMA((9,)),
+            pltpu.SemaphoreType.DMA((8,)),
+            pltpu.SemaphoreType.DMA((8,)),
             pltpu.SemaphoreType.DMA((2,)),
         ],
         compiler_params=pltpu.CompilerParams(collective_id=0, has_side_effects=True),

time: 88.1 us -> 79.7 us (0.905)
  Pallas kernels: 84.4 us -> 77.3 us
  local copies, waits for them, and re-layouts: 2.9 us -> 1.57 us
    pallas_call x1, Pallas kernels: 84.4 us -> 77.3 us  [local(): pl.pallas_call(functools.partial(kernel, tiles), out_shape=tuple((vm(a.sh...]
    unnamed x4 -> x2, local copies, waits for them, and re-layouts: 2.9 us -> 1.57 us
where the time goes in v2:
time: 79.7 us; the launch traced here: 79.5 us
  Pallas kernels  77.3 us (97%)
  local copies, waits for them, and re-layouts  1.57 us (2%)
    pallas_call x1, Pallas kernels, local(): pl.pallas_call(functools.partial(kernel, tiles), out_shape=tuple((vm(a.sh...  77.3 us

profile of v2, /device:TPU:16, one launch (start us, length us, event | category | flops | bytes accessed | tf_op | source)
XLA Modules:
  0.0 79.5 jit_solution(3561698667948576512)
XLA Ops:
  0.6 77.3 %modal_backward.1 = (bf16[1,128,4096]{2,1,0:T(8,128)(2,1)S(1)}, f32[8,256]{1,0:T(8,128)S(1)}) custom-call(f32[8]{0:T(128)} %rates.1, bf16[1,128,4096]{2,1,0:T(8,128)(2,1)} %g_hbm.1, bf16[1,128,4096]{2,1,0:T(8,128)(2,1)} %x_hbm.1, f32[8,4096]{1,0:T(8,128)} %res_hbm.1), custom_call_target="tpu_custom_call" | custom-call | tf_op jit(solution)/shard_map/modal_backward/pallas_call | solution.py:287
  77.9 1.0 %copy.8 = bf16[1,128,4096]{2,1,0:T(8,128)(2,1)} copy(bf16[1,128,4096]{2,1,0:T(8,128)(2,1)S(1)} %get-tuple-element.2) | data formatting | bytes 2097152
  78.9 0.6 copy.9

commit v3 on v2

v3 whole, which is shorter than its diff:
```python
import functools

import jax
import jax.numpy as jnp
from jax import lax
from jax.experimental import pallas as pl
from jax.experimental.pallas import tpu as pltpu
from jax.sharding import PartitionSpec as P

MESH = pl.DeviceIdType.MESH
F32 = jnp.float32
BF16 = jnp.bfloat16


def kernel(
    tiles, cube, rates, g_hbm, x_hbm, res_hbm, gin_ref, rgrad_ref,
    g, x, res, dt, lg, s_out, w_out, l_out, l_in, s1, w1, intra, a_out, a_in, b_out, b_in,
    e_out, e_in, inc_out, inc_in, tw_out, tw_in, x_out, x_in, lsum, lz_in, r_out, r_in,
    in_sem, snd, rcv, r_rcv, far_sem,
):
    modes, rows = 8, 128
    cubes = tiles // cube
    near = tiles // 4
    d = lax.axis_index("dp")
    seq = lax.axis_index("seq")
    h, z = lax.div(seq, tiles), lax.rem(seq, tiles)
    p = 2 * d + h
    e, q = lax.div(z, cube), lax.rem(z, cube)
    tile = q * cubes + e
    owner = lax.div(tile, 2) == d
    S, W, LP, A, B, E, INC, TW, X, LZ, R = range(11)

    def wrap(v, n=tiles):
        return lax.rem(v + n, n)

    def line(zz):
        return (d, h * tiles + zz)

    def plane(pp):
        return (lax.div(pp, 2), lax.rem(pp, 2) * tiles + z)

    def send(kind, src, dst, dev):
        pltpu.make_async_remote_copy(
            src_ref=src, dst_ref=dst, send_sem=snd.at[kind], recv_sem=rcv.at[kind],
            device_id=dev, device_id_type=MESH,
        ).start()

    def wait_tiles(buf, sem, lo, n):
        part = buf.at[pl.ds(lo, n)]
        pltpu.make_async_copy(part, part, sem).wait()

    def got(kind, buf):
        wait_tiles(buf, rcv.at[kind], 1, buf.shape[0] - 1)

    copy_g = pltpu.make_async_copy(g_hbm.at[0], g, in_sem.at[0])
    copy_x = pltpu.make_async_copy(x_hbm.at[0], x, in_sem.at[1])
    copy_r = pltpu.make_async_copy(res_hbm, res, in_sem.at[2])
    copy_g.start()
    copy_x.start()
    copy_r.start()

    barrier = pltpu.get_barrier_semaphore()

    def greet_line(i, c):
        n = near - i
        for to in (wrap(z + n), wrap(z - n)):
            pl.semaphore_signal(barrier, inc=1, device_id=line(to), device_id_type=MESH)
        return c

    def greet_plane(j, c):
        to = plane(wrap(p + j))
        pl.semaphore_signal(barrier, inc=1, device_id=to, device_id_type=MESH)
        return c

    lax.fori_loop(0, near, greet_line, 0)
    lax.fori_loop(1, tiles, greet_plane, 0)

    mode_row = lax.broadcasted_iota(jnp.int32, (modes, 128), 0)
    rate = jnp.zeros((modes, 128), F32)
    for r in range(modes):
        rate = jnp.where(mode_row == r, rates[r], rate)
    gain = jnp.sqrt(1.0 - jnp.exp(-2.0 * rate))
    pos = lax.broadcasted_iota(jnp.int32, (modes, 128), 1).astype(F32)
    state_table = jnp.exp(-rate * pos).astype(BF16)
    carry_t = (gain * jnp.exp(-rate * (rows - pos))).astype(BF16)
    decay = jnp.exp(-rate * float(rows))
    decay_cube = jnp.exp(-rate * float(rows * cube))

    copy_g.wait()
    copy_x.wait()

    def states(i, c):
        cols = pl.ds(pl.multiple_of(i * 256, 256), 256)
        s = jnp.dot(state_table, g[:, cols], preferred_element_type=F32)
        w = jnp.dot(carry_t, x[:, cols], preferred_element_type=F32)
        for t in range(2):
            s_out[2 * i + t] = s[:, t * 128:(t + 1) * 128]
            w_out[2 * i + t] = w[:, t * 128:(t + 1) * 128]
        return c

    lax.fori_loop(0, tiles // 2, states, 0)

    pl.semaphore_wait(barrier, 2 * near + tiles - 1)
    for to in (wrap(z + near), wrap(z - near)):
        pl.semaphore_signal(far_sem, inc=1, device_id=line(to), device_id_type=MESH)

    for kind, src, dst in ((S, s_out, s1), (W, w_out, w1)):
        for n in range(1, cube):
            to = wrap(q + n, cube)
            block = pl.ds(to * cubes, cubes)
            send(kind, src.at[block], dst.at[cube - n], line(e * cube + to))
        dst[0] = src[pl.ds(q * cubes, cubes)]

    lag = (
        lax.broadcasted_iota(jnp.int32, (rows, rows), 1)
        - lax.broadcasted_iota(jnp.int32, (rows, rows), 0)
    ).astype(F32)
    causal = lag >= 0
    lag = jnp.maximum(lag, 0.0)
    for r in range(modes):
        full = jnp.full((rows, rows), rates[r], F32)
        gain_r = jnp.sqrt(1.0 - jnp.exp(-2.0 * full))
        dt[r] = jnp.where(causal, gain_r * jnp.exp(-full * lag), 0.0).astype(BF16)

    copy_r.wait()

    def local(i, c):
        cols = pl.ds(pl.multiple_of(i * 256, 256), 256)
        gc = g[:, cols]
        xc = x[:, cols].astype(F32)
        total = jnp.zeros((rows, 256), F32)
        sums = []
        for r in range(modes):
            v = jnp.dot(dt[r], gc, preferred_element_type=F32)
            total = total + v * res[r:r + 1, cols]
            sums.append(jnp.sum(v * xc, axis=0, keepdims=True))
        lg[:, cols] = total
        lp = jnp.concatenate(sums, axis=0)
        for t in range(2):
            l_out[2 * i + t] = lp[:, t * 128:(t + 1) * 128]
        return c

    lax.fori_loop(0, tiles // 2, local, 0)

    def send_l(j, c):
        to = wrap(p + j)
        pair = pl.ds(2 * lax.div(to, 2), 2)
        send(LP, l_out.at[pair], l_in.at[tiles - j], plane(to))
        return c

    lax.fori_loop(1, tiles, send_l, 0)

    got(S, s1)
    f = jnp.zeros((cubes, modes, 128), F32)
    for j in reversed(range(cube)):
        intra[j] = f
        f = s1[wrap(j - q, cube)] + decay[None] * f
    a_out[...] = f

    pl.semaphore_wait(far_sem, 2)

    def far_first(i):
        m = lax.div(i, 2)
        return cubes // 2 + jnp.where(lax.rem(i, 2) == 0, m, -m)

    def send_a(i, c):
        n = far_first(i)
        to = wrap(e + n, cubes)
        send(A, a_out.at[to], a_in.at[cubes - n], line(to * cube + q))
        return c

    lax.fori_loop(1, cubes, send_a, 0)
    a_in[0] = a_out[e]

    got(W, w1)
    weight = jnp.zeros((cubes, modes, 128), F32)
    cross = jnp.zeros((cubes, modes, 128), F32)
    for j in range(cube):
        wj = w1[wrap(j - q, cube)]
        weight = wj + decay[None] * weight
        cross = cross + intra[j] * wj
    for t in range(cubes):
        b_out[t, 0] = weight[t]
        b_out[t, 1] = cross[t]

    def send_b(i, c):
        n = far_first(i)
        to = wrap(e + n, cubes)
        send(B, b_out.at[to], b_in.at[cubes - n], line(to * cube + q))
        return c

    lax.fori_loop(1, cubes, send_b, 0)
    b_in[0] = b_out[e]

    got(LP, l_in)
    lsum[...] = l_out[pl.ds(2 * d, 2)] + jnp.sum(l_in[1:tiles], axis=0)

    def home(k):
        return lax.rem(k, cubes) * cube + lax.div(k, cubes)

    for i in range(2):
        to = home(2 * d + i)

        @pl.when(to != z)
        def _(i=i, to=to):
            send(LZ, lsum.at[i], lz_in.at[wrap(z - to)], line(to))

    got(A, a_in)

    def scan(f, keep):
        for c in reversed(range(cubes)):
            slot = wrap(c - e, cubes)
            if keep:
                e_out[slot] = f
            f = a_in[slot] + decay_cube * f
        return f

    tw_out[0] = scan(jnp.zeros((modes, 128), F32), False)
    send(TW, tw_out.at[0], tw_in.at[0], plane(p + 1 - 2 * h))
    wait_tiles(tw_in, rcv.at[TW], 0, 1)
    scan(jnp.where(h == 0, tw_in[0], 0.0), True)

    def send_e(i, c):
        n = far_first(i)
        to = wrap(e + n, cubes)
        send(E, e_out.at[n], e_in.at[cubes - n], line(to * cube + q))
        return c

    lax.fori_loop(1, cubes, send_e, 0)
    e_in[0] = e_out[0]

    got(B, b_in)
    total = jnp.zeros((modes, 128), F32)
    for slot in range(cubes):
        total = total + b_in[slot, 1] + e_out[slot] * b_in[slot, 0]
    x_out[0] = total
    to_p = 2 * lax.div(tile, 2)
    for half in range(2):
        to = to_p + half

        @pl.when(to != p)
        def _(to=to):
            send(X, x_out.at[0], x_in.at[wrap(p - to)], plane(to))

    @pl.when(owner)
    def _():
        got(LZ, lz_in)
        got(X, x_in)
        r_out[0] = (
            lsum[lax.rem(tile, 2)] + jnp.sum(lz_in[1:tiles], axis=0)
            + x_out[0] + jnp.sum(x_in[1:tiles], axis=0)
        )

        def send_r(i, c):
            m = lax.div(i, 2)
            n = tiles // 2 + jnp.where(lax.rem(i, 2) == 0, m, -m)
            side = lax.rem(tile, 2)
            pltpu.make_async_remote_copy(
                src_ref=r_out.at[0], dst_ref=r_in.at[side],
                send_sem=snd.at[R], recv_sem=r_rcv.at[side],
                device_id=line(wrap(z + n)), device_id_type=MESH,
            ).start()
            return c

        lax.fori_loop(1, tiles, send_r, 0)

    got(E, e_in)
    for t in range(cubes):
        v = e_in[wrap(t - e, cubes)]
        for j in reversed(range(cube)):
            inc_out[wrap(j - q, cube), t] = intra[j, t] + v
            v = decay * v
    for n in range(1, cube):
        to = wrap(q + n, cube)
        send(INC, inc_out.at[n], inc_in.at[cube - n], line(e * cube + to))
    inc_in[0] = inc_out[0]

    col = lax.rem(lax.broadcasted_iota(jnp.int32, (rows, 32), 1), modes)
    part = lax.div(lax.broadcasted_iota(jnp.int32, (rows, 32), 1), modes)
    at = lax.broadcasted_iota(jnp.int32, (rows, 32), 0).astype(F32)
    rate_c = jnp.zeros((rows, 32), F32)
    for r in range(modes):
        rate_c = jnp.where(col == r, rates[r], rate_c)
    gain_c = jnp.sqrt(1.0 - jnp.exp(-2.0 * rate_c))
    carry3 = jnp.where(part < 3, gain_c * jnp.exp(-rate_c * (rows - at)), 0.0).astype(BF16)

    got(INC, inc_in)

    def finish(i, c):
        cols = pl.ds(pl.multiple_of(i * 256, 256), 256)
        slot = wrap(lax.div(2 * i, cubes) - q, cube)
        t = lax.rem(2 * i, cubes)
        inc = jnp.concatenate([inc_in[slot, t], inc_in[slot, t + 1]], axis=1)
        u = inc * res[:, cols]
        u0 = u.astype(BF16).astype(F32)
        u1 = (u - u0).astype(BF16).astype(F32)
        u2 = u - u0 - u1
        u3 = jnp.concatenate([u0, u1, u2, jnp.zeros_like(u)], axis=0).astype(BF16)
        out = lg[:, cols] + jnp.dot(carry3, u3, preferred_element_type=F32)
        gin_ref[0, :, cols] = out.astype(BF16)
        return c

    lax.fori_loop(0, tiles // 2, finish, 0)

    for i in range(2):
        mine = 2 * d + i == tile

        @pl.when(jnp.logical_not(mine))
        def _(i=i):
            wait_tiles(r_in, r_rcv.at[i], i, 1)
            rgrad_ref[:, i * 128:(i + 1) * 128] = r_in[i]

        @pl.when(mine)
        def _(i=i):
            rgrad_ref[:, i * 128:(i + 1) * 128] = r_out[0]

    drains = ((S, s1), (W, w1), (LP, l_in), (A, a_in), (B, b_in), (E, e_in), (INC, inc_in))
    for kind, buf in drains:
        wait_tiles(buf, snd.at[kind], 1, buf.shape[0] - 1)
    wait_tiles(tw_in, snd.at[TW], 0, 1)
    for i in range(2):
        @pl.when(home(2 * d + i) != z)
        def _():
            wait_tiles(lsum, snd.at[LZ], 0, 1)
    for half in range(2):
        @pl.when(to_p + half != p)
        def _():
            wait_tiles(x_out, snd.at[X], 0, 1)

    @pl.when(owner)
    def _():
        wait_tiles(lz_in, snd.at[R], 1, tiles - 1)


def local(grad_out, block_in, residues, decay_rates):
    _, rows, channels = grad_out.shape
    tiles = channels // 128
    modes = residues.shape[0]
    vm = pltpu.VMEM
    cube = 4 if tiles % 8 == 0 else 2
    cubes = tiles // cube

    def held(*lead):
        return vm((*lead, modes, 128), F32)

    anywhere = pl.BlockSpec(memory_space=pl.ANY)
    shapes = (
        jax.ShapeDtypeStruct((1, rows, channels), BF16),
        jax.ShapeDtypeStruct((modes, 256), F32),
    )
    return pl.pallas_call(
        functools.partial(kernel, tiles, cube),
        out_shape=tuple(vm(a.shape, a.dtype) for a in shapes),
        in_specs=[pl.BlockSpec(memory_space=pltpu.SMEM), anywhere, anywhere, anywhere],
        out_specs=(pl.BlockSpec(memory_space=pltpu.VMEM), pl.BlockSpec(memory_space=pltpu.VMEM)),
        scratch_shapes=[
            vm((rows, channels), BF16),
            vm((rows, channels), BF16),
            vm((modes, channels), F32),
            vm((modes, rows, rows), BF16),
            vm((rows, channels), F32),
            held(tiles), held(tiles), held(tiles), held(tiles, 2),
            held(cube, cubes), held(cube, cubes), held(cube, cubes),
            held(cubes), held(cubes), held(cubes, 2), held(cubes, 2),
            held(cubes), held(cubes), held(cube, cubes), held(cube, cubes),
            held(1), held(1), held(1), held(tiles), held(2), held(tiles), held(1), held(2),
            pltpu.SemaphoreType.DMA((3,)),
            pltpu.SemaphoreType.DMA((11,)),
            pltpu.SemaphoreType.DMA((11,)),
            pltpu.SemaphoreType.DMA((2,)),
            pltpu.SemaphoreType.REGULAR,
        ],
        compiler_params=pltpu.CompilerParams(collective_id=0, has_side_effects=True),
        name="modal_backward",
    )(decay_rates, grad_out, block_in, residues)


def solution(mesh):
    placed = (P("dp", "seq", None), P("dp", "seq", None), P(), P())
    return jax.shard_map(
        local,
        mesh=mesh,
        in_specs=placed,
        out_specs=(P("dp", "seq", None), P(None, "dp")),
        check_vma=False,
    )
```

time: 79.7 us -> 67.9 us (0.85)
  the two profiles are of different devices: /device:TPU:16 before, /device:TPU:8 now
where the time goes in v3:
time: 67.9 us; the launch traced here: 67.8 us
  Pallas kernels  65.6 us (97%)
  local copies, waits for them, and re-layouts  1.57 us (2%)
    pallas_call x1, Pallas kernels, local(): pl.pallas_call(functools.partial(kernel, tiles, cube), out_shape=tuple((v...  65.6 us
    unnamed x2, local copies, waits for them, and re-layouts  1.57 us

profile of v3, /device:TPU:8, one launch (start us, length us, event | category | flops | bytes accessed | tf_op | source)
XLA Modules:
  0.0 67.8 jit_solution(17737989631047805129)
XLA Ops:
  0.6 65.6 %modal_backward.1 = (bf16[1,128,4096]{2,1,0:T(8,128)(2,1)S(1)}, f32[8,256]{1,0:T(8,128)S(1)}) custom-call(f32[8]{0:T(128)} %rates.1, bf16[1,128,4096]{2,1,0:T(8,128)(2,1)} %g_hbm.1, bf16[1,128,4096]{2,1,0:T(8,128)(2,1)} %x_hbm.1, f32[8,4096]{1,0:T(8,128)} %res_hbm.1), custom_call_target="tpu_custom_call" | custom-call | tf_op jit(solution)/shard_map/modal_backward/pallas_call | solution.py:351
  66.2 1.0 %copy.8 = bf16[1,128,4096]{2,1,0:T(8,128)(2,1)} copy(bf16[1,128,4096]{2,1,0:T(8,128)(2,1)S(1)} %get-tuple-element.2) | data formatting | bytes 2097152
  67.2 0.6 copy.9

commit v4 on v3

--- a/solution.py
+++ b/solution.py
@@ -16,7 +16,7 @@
     tiles, cube, rates, g_hbm, x_hbm, res_hbm, gin_ref, rgrad_ref,
     g, x, res, dt, lg, s_out, w_out, l_out, l_in, s1, w1, intra, a_out, a_in, b_out, b_in,
     e_out, e_in, inc_out, inc_in, tw_out, tw_in, x_out, x_in, lsum, lz_in, r_out, r_in,
-    in_sem, snd, rcv, r_rcv, far_sem,
+    in_sem, snd, rcv, r_rcv, e_rcv, inc_rcv, far_sem,
 ):
     modes, rows = 8, 128
     cubes = tiles // cube
@@ -104,12 +104,14 @@
     for to in (wrap(z + near), wrap(z - near)):
         pl.semaphore_signal(far_sem, inc=1, device_id=line(to), device_id_type=MESH)
 
-    for kind, src, dst in ((S, s_out, s1), (W, w_out, w1)):
+    def level_1(kind, src, dst):
         for n in range(1, cube):
             to = wrap(q + n, cube)
             block = pl.ds(to * cubes, cubes)
             send(kind, src.at[block], dst.at[cube - n], line(e * cube + to))
         dst[0] = src[pl.ds(q * cubes, cubes)]
+
+    level_1(S, s_out, s1)
 
     lag = (
         lax.broadcasted_iota(jnp.int32, (rows, rows), 1)
@@ -140,15 +142,9 @@
             l_out[2 * i + t] = lp[:, t * 128:(t + 1) * 128]
         return c
 
-    lax.fori_loop(0, tiles // 2, local, 0)
-
-    def send_l(j, c):
-        to = wrap(p + j)
-        pair = pl.ds(2 * lax.div(to, 2), 2)
-        send(LP, l_out.at[pair], l_in.at[tiles - j], plane(to))
-        return c
-
-    lax.fori_loop(1, tiles, send_l, 0)
+    lax.fori_loop(0, tiles // 4, local, 0)
+    level_1(W, w_out, w1)
+    lax.fori_loop(tiles // 4, tiles // 2, local, 0)
 
     got(S, s1)
     f = jnp.zeros((cubes, modes, 128), F32)
@@ -179,9 +175,7 @@
         wj = w1[wrap(j - q, cube)]
         weight = wj + decay[None] * weight
         cross = cross + intra[j] * wj
-    for t in range(cubes):
-        b_out[t, 0] = weight[t]
-        b_out[t, 1] = cross[t]
+    b_out[...] = weight
 
     def send_b(i, c):
         n = far_first(i)
@@ -191,6 +185,17 @@
 
     lax.fori_loop(1, cubes, send_b, 0)
     b_in[0] = b_out[e]
+
+    mine = pl.ds(q * cubes, cubes)
+    l_out[mine] = l_out[mine] + cross
+
+    def send_l(j, c):
+        to = wrap(p + j)
+        pair = pl.ds(2 * lax.div(to, 2), 2)
+        send(LP, l_out.at[pair], l_in.at[tiles - j], plane(to))
+        return c
+
+    lax.fori_loop(1, tiles, send_l, 0)
 
     got(LP, l_in)
     lsum[...] = l_out[pl.ds(2 * d, 2)] + jnp.sum(l_in[1:tiles], axis=0)
@@ -223,7 +228,11 @@
     def send_e(i, c):
         n = far_first(i)
         to = wrap(e + n, cubes)
-        send(E, e_out.at[n], e_in.at[cubes - n], line(to * cube + q))
+        pltpu.make_async_remote_copy(
+            src_ref=e_out.at[n], dst_ref=e_in.at[cubes - n],
+            send_sem=snd.at[E], recv_sem=e_rcv.at[cubes - n],
+            device_id=line(to * cube + q), device_id_type=MESH,
+        ).start()
         return c
 
     lax.fori_loop(1, cubes, send_e, 0)
@@ -232,7 +241,7 @@
     got(B, b_in)
     total = jnp.zeros((modes, 128), F32)
     for slot in range(cubes):
-        total = total + b_in[slot, 1] + e_out[slot] * b_in[slot, 0]
+        total = total + e_out[slot] * b_in[slot]
     x_out[0] = total
     to_p = 2 * lax.div(tile, 2)
     for half in range(2):
@@ -264,17 +273,6 @@
 
         lax.fori_loop(1, tiles, send_r, 0)
 
-    got(E, e_in)
-    for t in range(cubes):
-        v = e_in[wrap(t - e, cubes)]
-        for j in reversed(range(cube)):
-            inc_out[wrap(j - q, cube), t] = intra[j, t] + v
-            v = decay * v
-    for n in range(1, cube):
-        to = wrap(q + n, cube)
-        send(INC, inc_out.at[n], inc_in.at[cube - n], line(e * cube + to))
-    inc_in[0] = inc_out[0]
-
     col = lax.rem(lax.broadcasted_iota(jnp.int32, (rows, 32), 1), modes)
     part = lax.div(lax.broadcasted_iota(jnp.int32, (rows, 32), 1), modes)
     at = lax.broadcasted_iota(jnp.int32, (rows, 32), 0).astype(F32)
@@ -284,23 +282,40 @@
     gain_c = jnp.sqrt(1.0 - jnp.exp(-2.0 * rate_c))
     carry3 = jnp.where(part < 3, gain_c * jnp.exp(-rate_c * (rows - at)), 0.0).astype(BF16)
 
-    got(INC, inc_in)
-
-    def finish(i, c):
-        cols = pl.ds(pl.multiple_of(i * 256, 256), 256)
-        slot = wrap(lax.div(2 * i, cubes) - q, cube)
-        t = lax.rem(2 * i, cubes)
-        inc = jnp.concatenate([inc_in[slot, t], inc_in[slot, t + 1]], axis=1)
-        u = inc * res[:, cols]
-        u0 = u.astype(BF16).astype(F32)
-        u1 = (u - u0).astype(BF16).astype(F32)
-        u2 = u - u0 - u1
-        u3 = jnp.concatenate([u0, u1, u2, jnp.zeros_like(u)], axis=0).astype(BF16)
-        out = lg[:, cols] + jnp.dot(carry3, u3, preferred_element_type=F32)
-        gin_ref[0, :, cols] = out.astype(BF16)
-        return c
-
-    lax.fori_loop(0, tiles // 2, finish, 0)
+    order = sorted(range(cubes), key=lambda n: min(n, cubes - n))
+    for n in order:
+        if n:
+            wait_tiles(e_in, e_rcv.at[n], n, 1)
+        t = wrap(e + n, cubes)
+        v = e_in[n]
+        for j in reversed(range(cube)):
+            inc_out[n, wrap(j - q, cube)] = intra[j, t] + v
+            v = decay * v
+        for m in range(1, cube):
+            pltpu.make_async_remote_copy(
+                src_ref=inc_out.at[n, m], dst_ref=inc_in.at[n, cube - m],
+                send_sem=snd.at[INC], recv_sem=inc_rcv.at[n],
+                device_id=line(e * cube + wrap(q + m, cube)), device_id_type=MESH,
+            ).start()
+        inc_in[n, 0] = inc_out[n, 0]
+
+    for n in order:
+        wait_tiles(inc_in.at[n], inc_rcv.at[n], 1, cube - 1)
+        t = wrap(e + n, cubes)
+
+        def finish(m, c, n=n, t=t):
+            k = wrap(q + m, cube) * cubes + t
+            cols = pl.ds(pl.multiple_of(k * 128, 128), 128)
+            u = inc_in[n, m] * res[:, cols]
+            u0 = u.astype(BF16).astype(F32)
+            u1 = (u - u0).astype(BF16).astype(F32)
+            u2 = u - u0 - u1
+            u3 = jnp.concatenate([u0, u1, u2, jnp.zeros_like(u)], axis=0).astype(BF16)
+            out = lg[:, cols] + jnp.dot(carry3, u3, preferred_element_type=F32)
+            gin_ref[0, :, cols] = out.astype(BF16)
+            return c
+
+        lax.fori_loop(0, cube, finish, 0, unroll=2)
 
     for i in range(2):
         mine = 2 * d + i == tile
@@ -314,9 +329,10 @@
         def _(i=i):
             rgrad_ref[:, i * 128:(i + 1) * 128] = r_out[0]
 
-    drains = ((S, s1), (W, w1), (LP, l_in), (A, a_in), (B, b_in), (E, e_in), (INC, inc_in))
+    drains = ((S, s1), (W, w1), (LP, l_in), (A, a_in), (B, b_in), (E, e_in))
     for kind, buf in drains:
         wait_tiles(buf, snd.at[kind], 1, buf.shape[0] - 1)
+    wait_tiles(l_in, snd.at[INC], 0, cubes * (cube - 1) // 2)
     wait_tiles(tw_in, snd.at[TW], 0, 1)
     for i in range(2):
         @pl.when(home(2 * d + i) != z)
@@ -332,6 +348,17 @@
         wait_tiles(lz_in, snd.at[R], 1, tiles - 1)
 
 
+def write_out(gin, rgrad, gin_hbm, rgrad_hbm, sem):
+    copies = [
+        pltpu.make_async_copy(gin, gin_hbm, sem.at[0]),
+        pltpu.make_async_copy(rgrad, rgrad_hbm, sem.at[1]),
+    ]
+    for copy in copies:
+        copy.start()
+    for copy in copies:
+        copy.wait()
+
+
 def local(grad_out, block_in, residues, decay_rates):
     _, rows, channels = grad_out.shape
     tiles = channels // 128
@@ -348,7 +375,7 @@
         jax.ShapeDtypeStruct((1, rows, channels), BF16),
         jax.ShapeDtypeStruct((modes, 256), F32),
     )
-    return pl.pallas_call(
+    kept = pl.pallas_call(
         functools.partial(kernel, tiles, cube),
         out_shape=tuple(vm(a.shape, a.dtype) for a in shapes),
         in_specs=[pl.BlockSpec(memory_space=pltpu.SMEM), anywhere, anywhere, anywhere],
@@ -361,18 +388,31 @@
             vm((rows, channels), F32),
             held(tiles), held(tiles), held(tiles), held(tiles, 2),
             held(cube, cubes), held(cube, cubes), held(cube, cubes),
-            held(cubes), held(cubes), held(cubes, 2), held(cubes, 2),
-            held(cubes), held(cubes), held(cube, cubes), held(cube, cubes),
+            held(cubes), held(cubes), held(cubes), held(cubes),
+            held(cubes), held(cubes), held(cubes, cube), held(cubes, cube),
             held(1), held(1), held(1), held(tiles), held(2), held(tiles), held(1), held(2),
             pltpu.SemaphoreType.DMA((3,)),
             pltpu.SemaphoreType.DMA((11,)),
             pltpu.SemaphoreType.DMA((11,)),
             pltpu.SemaphoreType.DMA((2,)),
+            pltpu.SemaphoreType.DMA((cubes,)),
+            pltpu.SemaphoreType.DMA((cubes,)),
             pltpu.SemaphoreType.REGULAR,
         ],
         compiler_params=pltpu.CompilerParams(collective_id=0, has_side_effects=True),
         name="modal_backward",
     )(decay_rates, grad_out, block_in, residues)
+    in_vmem = pl.BlockSpec(memory_space=pltpu.VMEM)
+    kept = tuple(pltpu.with_memory_space_constraint(a, pltpu.VMEM) for a in kept)
+    return pl.pallas_call(
+        write_out,
+        out_shape=shapes,
+        in_specs=[in_vmem, in_vmem],
+        out_specs=(anywhere, anywhere),
+        scratch_shapes=[pltpu.SemaphoreType.DMA((2,))],
+        compiler_params=pltpu.CompilerParams(vmem_limit_bytes=1 << 20),
+        name="write_out",
+    )(*kept)
 
 
 def solution(mesh):

time: 67.9 us -> 64.4 us (0.948)
  the two profiles are of different devices: /device:TPU:8 before, /device:TPU:6 now
where the time goes in v4:
time: 64.4 us; the launch traced here: 64.2 us
  Pallas kernels  63.6 us (99%)
    pallas_call x1, Pallas kernels, local(): pl.pallas_call(functools.partial(kernel, tiles, cube), out_shape=tuple((v...  62.6 us

profile of v4, /device:TPU:6, one launch (start us, length us, event | category | flops | bytes accessed | tf_op | source)
XLA Modules:
  0.0 64.2 jit_solution(18320312582680230349)
XLA Ops:
  0.6 62.6 %modal_backward.1 = (bf16[1,128,4096]{2,1,0:T(8,128)(2,1)S(1)}, f32[8,256]{1,0:T(8,128)S(1)}) custom-call(f32[8]{0:T(128)} %rates.1, bf16[1,128,4096]{2,1,0:T(8,128)(2,1)} %g_hbm.1, bf16[1,128,4096]{2,1,0:T(8,128)(2,1)} %x_hbm.1, f32[8,4096]{1,0:T(8,128)} %res_hbm.1), custom_call_target="tpu_custom_call" | custom-call | tf_op jit(solution)/shard_map/modal_backward/pallas_call | solution.py:378
  63.2 1.0 %write_out.1 = (bf16[1,128,4096]{2,1,0:T(8,128)(2,1)}, f32[8,256]{1,0:T(8,128)}) custom-call(bf16[1,128,4096]{2,1,0:T(8,128)(2,1)S(1)} %get-tuple-element.4.gin, f32[8,256]{1,0:T(8,128)S(1)} %get-tuple-element.5.rgrad), custom_call_target="tpu_custom_call" | custom-call | tf_op jit(solution)/shard_map/write_out/pallas_call | solution.py:407

commit v5 on v4

--- a/solution.py
+++ b/solution.py
@@ -15,8 +15,8 @@
 def kernel(
     tiles, cube, rates, g_hbm, x_hbm, res_hbm, gin_ref, rgrad_ref,
     g, x, res, dt, lg, s_out, w_out, l_out, l_in, s1, w1, intra, a_out, a_in, b_out, b_in,
-    e_out, e_in, inc_out, inc_in, tw_out, tw_in, x_out, x_in, lsum, lz_in, r_out, r_in,
-    in_sem, snd, rcv, r_rcv, e_rcv, inc_rcv, far_sem,
+    e_out, e_in, inc_out, inc_in, tw_out, f_in, x_out, x_in, lsum, lz_in, r_out, r_in,
+    in_sem, snd, rcv, r_rcv, e_rcv, inc_rcv, f_rcv, far_sem,
 ):
     modes, rows = 8, 128
     cubes = tiles // cube
@@ -26,7 +26,11 @@
     h, z = lax.div(seq, tiles), lax.rem(seq, tiles)
     p = 2 * d + h
     e, q = lax.div(z, cube), lax.rem(z, cube)
-    tile = q * cubes + e
+
+    def place(c):
+        return c + 2 * lax.div(c, 4) - 4 * lax.div(c, 6)
+
+    tile = q * cubes + place(e)
     owner = lax.div(tile, 2) == d
     S, W, LP, A, B, E, INC, TW, X, LZ, R = range(11)
 
@@ -153,20 +157,23 @@
         f = s1[wrap(j - q, cube)] + decay[None] * f
     a_out[...] = f
 
+    def send_a(n):
+        to = wrap(e + n, cubes)
+        send(A, a_out.at[place(to)], a_in.at[cubes - n], line(to * cube + q))
+
+    def apart(n):
+        return cube * min(n, cubes - n)
+
+    by_distance = sorted(range(1, cubes), key=apart, reverse=True)
+    for n in by_distance:
+        if apart(n) <= near:
+            send_a(n)
+
     pl.semaphore_wait(far_sem, 2)
-
-    def far_first(i):
-        m = lax.div(i, 2)
-        return cubes // 2 + jnp.where(lax.rem(i, 2) == 0, m, -m)
-
-    def send_a(i, c):
-        n = far_first(i)
-        to = wrap(e + n, cubes)
-        send(A, a_out.at[to], a_in.at[cubes - n], line(to * cube + q))
-        return c
-
-    lax.fori_loop(1, cubes, send_a, 0)
-    a_in[0] = a_out[e]
+    for n in by_distance:
+        if apart(n) > near:
+            send_a(n)
+    a_in[0] = a_out[place(e)]
 
     got(W, w1)
     weight = jnp.zeros((cubes, modes, 128), F32)
@@ -177,14 +184,18 @@
         cross = cross + intra[j] * wj
     b_out[...] = weight
 
+    def far_first(i):
+        m = lax.div(i, 2)
+        return cubes // 2 + jnp.where(lax.rem(i, 2) == 0, m, -m)
+
     def send_b(i, c):
         n = far_first(i)
         to = wrap(e + n, cubes)
-        send(B, b_out.at[to], b_in.at[cubes - n], line(to * cube + q))
+        send(B, b_out.at[place(to)], b_in.at[cubes - n], line(to * cube + q))
         return c
 
     lax.fori_loop(1, cubes, send_b, 0)
-    b_in[0] = b_out[e]
+    b_in[0] = b_out[place(e)]
 
     mine = pl.ds(q * cubes, cubes)
     l_out[mine] = l_out[mine] + cross
@@ -201,7 +212,7 @@
     lsum[...] = l_out[pl.ds(2 * d, 2)] + jnp.sum(l_in[1:tiles], axis=0)
 
     def home(k):
-        return lax.rem(k, cubes) * cube + lax.div(k, cubes)
+        return place(lax.rem(k, cubes)) * cube + lax.div(k, cubes)
 
     for i in range(2):
         to = home(2 * d + i)
@@ -220,10 +231,23 @@
             f = a_in[slot] + decay_cube * f
         return f
 
-    tw_out[0] = scan(jnp.zeros((modes, 128), F32), False)
-    send(TW, tw_out.at[0], tw_in.at[0], plane(p + 1 - 2 * h))
-    wait_tiles(tw_in, rcv.at[TW], 0, 1)
-    scan(jnp.where(h == 0, tw_in[0], 0.0), True)
+    tw_out[0] = scan(jnp.zeros((modes, 128), F32), True)
+
+    @pl.when(h == 1)
+    def _():
+        f_in[...] = jnp.zeros_like(f_in)
+
+        def send_f(n, c):
+            to = wrap(e + n, cubes)
+            slot = wrap(-n, cubes)
+            pltpu.make_async_remote_copy(
+                src_ref=tw_out.at[0], dst_ref=f_in.at[slot],
+                send_sem=snd.at[TW], recv_sem=f_rcv.at[slot],
+                device_id=(d, to * cube + q), device_id_type=MESH,
+            ).start()
+            return c
+
+        lax.fori_loop(0, cubes, send_f, 0)
 
     def send_e(i, c):
         n = far_first(i)
@@ -242,6 +266,15 @@
     total = jnp.zeros((modes, 128), F32)
     for slot in range(cubes):
         total = total + e_out[slot] * b_in[slot]
+    reach = jnp.zeros((modes, 128), F32)
+    for c in range(cubes):
+        reach = b_in[wrap(c - e, cubes)] + decay_cube * reach
+
+    @pl.when(h == 0)
+    def _():
+        wait_tiles(f_in, f_rcv.at[0], 0, 1)
+
+    total = total + f_in[0] * reach
     x_out[0] = total
     to_p = 2 * lax.div(tile, 2)
     for half in range(2):
@@ -282,12 +315,18 @@
     gain_c = jnp.sqrt(1.0 - jnp.exp(-2.0 * rate_c))
     carry3 = jnp.where(part < 3, gain_c * jnp.exp(-rate_c * (rows - at)), 0.0).astype(BF16)
 
+    ahead = jnp.exp(-rate * (rows * cube * (cubes - 1 - e)).astype(F32))
     order = sorted(range(cubes), key=lambda n: min(n, cubes - n))
     for n in order:
         if n:
             wait_tiles(e_in, e_rcv.at[n], n, 1)
-        t = wrap(e + n, cubes)
-        v = e_in[n]
+
+            @pl.when(h == 0)
+            def _(n=n):
+                wait_tiles(f_in, f_rcv.at[n], n, 1)
+
+        t = place(wrap(e + n, cubes))
+        v = e_in[n] + ahead * f_in[n]
         for j in reversed(range(cube)):
             inc_out[n, wrap(j - q, cube)] = intra[j, t] + v
             v = decay * v
@@ -301,7 +340,7 @@
 
     for n in order:
         wait_tiles(inc_in.at[n], inc_rcv.at[n], 1, cube - 1)
-        t = wrap(e + n, cubes)
+        t = place(wrap(e + n, cubes))
 
         def finish(m, c, n=n, t=t):
             k = wrap(q + m, cube) * cubes + t
@@ -333,7 +372,11 @@
     for kind, buf in drains:
         wait_tiles(buf, snd.at[kind], 1, buf.shape[0] - 1)
     wait_tiles(l_in, snd.at[INC], 0, cubes * (cube - 1) // 2)
-    wait_tiles(tw_in, snd.at[TW], 0, 1)
+
+    @pl.when(h == 1)
+    def _():
+        wait_tiles(f_in, snd.at[TW], 0, cubes)
+
     for i in range(2):
         @pl.when(home(2 * d + i) != z)
         def _():
@@ -349,10 +392,14 @@
 
 
 def write_out(gin, rgrad, gin_hbm, rgrad_hbm, sem):
-    copies = [
-        pltpu.make_async_copy(gin, gin_hbm, sem.at[0]),
-        pltpu.make_async_copy(rgrad, rgrad_hbm, sem.at[1]),
-    ]
+    parts = sem.shape[0] - 1
+    size = gin.shape[1] // parts
+    copies = [pltpu.make_async_copy(rgrad, rgrad_hbm, sem.at[parts])]
+    for i in range(parts):
+        at = pl.ds(i * size, size)
+        copies.append(
+            pltpu.make_async_copy(gin.at[0, at], gin_hbm.at[0, at], sem.at[i])
+        )
     for copy in copies:
         copy.start()
     for copy in copies:
@@ -390,11 +437,12 @@
             held(cube, cubes), held(cube, cubes), held(cube, cubes),
             held(cubes), held(cubes), held(cubes), held(cubes),
             held(cubes), held(cubes), held(cubes, cube), held(cubes, cube),
-            held(1), held(1), held(1), held(tiles), held(2), held(tiles), held(1), held(2),
+            held(1), held(cubes), held(1), held(tiles), held(2), held(tiles), held(1), held(2),
             pltpu.SemaphoreType.DMA((3,)),
             pltpu.SemaphoreType.DMA((11,)),
             pltpu.SemaphoreType.DMA((11,)),
             pltpu.SemaphoreType.DMA((2,)),
+            pltpu.SemaphoreType.DMA((cubes,)),
             pltpu.SemaphoreType.DMA((cubes,)),
             pltpu.SemaphoreType.DMA((cubes,)),
             pltpu.SemaphoreType.REGULAR,
@@ -409,7 +457,7 @@
         out_shape=shapes,
         in_specs=[in_vmem, in_vmem],
         out_specs=(anywhere, anywhere),
-        scratch_shapes=[pltpu.SemaphoreType.DMA((2,))],
+        scratch_shapes=[pltpu.SemaphoreType.DMA((9,))],
         compiler_params=pltpu.CompilerParams(vmem_limit_bytes=1 << 20),
         name="write_out",
     )(*kept)

time: 64.4 us -> 63.8 us (level)
  the two profiles are of different devices: /device:TPU:6 before, /device:TPU:3 now
where the time goes in v5:
time: 63.8 us; the launch traced here: 63.6 us
  Pallas kernels  62.9 us (99%)
  between operations  0.64 us (1%)
    pallas_call x1, Pallas kernels, local(): pl.pallas_call(functools.partial(kernel, tiles, cube), out_shape=tuple((v...  61.9 us

profile of v5, /device:TPU:3, one launch (start us, length us, event | category | flops | bytes accessed | tf_op | source)
XLA Modules:
  0.0 63.6 jit_solution(18219175777031927961)
XLA Ops:
  0.6 61.9 %modal_backward.1 = (bf16[1,128,4096]{2,1,0:T(8,128)(2,1)S(1)}, f32[8,256]{1,0:T(8,128)S(1)}) custom-call(f32[8]{0:T(128)} %rates.1, bf16[1,128,4096]{2,1,0:T(8,128)(2,1)} %g_hbm.1, bf16[1,128,4096]{2,1,0:T(8,128)(2,1)} %x_hbm.1, f32[8,4096]{1,0:T(8,128)} %res_hbm.1), custom_call_target="tpu_custom_call" | custom-call | tf_op jit(solution)/shard_map/modal_backward/pallas_call | solution.py:425
  62.5 1.0 %write_out.1 = (bf16[1,128,4096]{2,1,0:T(8,128)(2,1)}, f32[8,256]{1,0:T(8,128)}) custom-call(bf16[1,128,4096]{2,1,0:T(8,128)(2,1)S(1)} %get-tuple-element.4.gin, f32[8,256]{1,0:T(8,128)S(1)} %get-tuple-element.5.rgrad), custom_call_target="tpu_custom_call" | custom-call | tf_op jit(solution)/shard_map/write_out/pallas_call | solution.py:455

commit v6 on v5

--- a/solution.py
+++ b/solution.py
@@ -59,9 +59,6 @@
     copy_g = pltpu.make_async_copy(g_hbm.at[0], g, in_sem.at[0])
     copy_x = pltpu.make_async_copy(x_hbm.at[0], x, in_sem.at[1])
     copy_r = pltpu.make_async_copy(res_hbm, res, in_sem.at[2])
-    copy_g.start()
-    copy_x.start()
-    copy_r.start()
 
     barrier = pltpu.get_barrier_semaphore()
 
@@ -77,6 +74,9 @@
         return c
 
     lax.fori_loop(0, near, greet_line, 0)
+    copy_g.start()
+    copy_x.start()
+    copy_r.start()
     lax.fori_loop(1, tiles, greet_plane, 0)
 
     mode_row = lax.broadcasted_iota(jnp.int32, (modes, 128), 0)
@@ -165,14 +165,9 @@
         return cube * min(n, cubes - n)
 
     by_distance = sorted(range(1, cubes), key=apart, reverse=True)
-    for n in by_distance:
-        if apart(n) <= near:
-            send_a(n)
-
     pl.semaphore_wait(far_sem, 2)
     for n in by_distance:
-        if apart(n) > near:
-            send_a(n)
+        send_a(n)
     a_in[0] = a_out[place(e)]
 
     got(W, w1)
@@ -338,6 +333,23 @@
             ).start()
         inc_in[n, 0] = inc_out[n, 0]
 
+    drains = ((S, s1), (W, w1), (LP, l_in), (A, a_in), (B, b_in), (E, e_in))
+    for kind, buf in drains:
+        wait_tiles(buf, snd.at[kind], 1, buf.shape[0] - 1)
+
+    @pl.when(h == 1)
+    def _():
+        wait_tiles(f_in, snd.at[TW], 0, cubes)
+
+    for i in range(2):
+        @pl.when(home(2 * d + i) != z)
+        def _():
+            wait_tiles(lsum, snd.at[LZ], 0, 1)
+    for half in range(2):
+        @pl.when(to_p + half != p)
+        def _():
+            wait_tiles(x_out, snd.at[X], 0, 1)
+
     for n in order:
         wait_tiles(inc_in.at[n], inc_rcv.at[n], 1, cube - 1)
         t = place(wrap(e + n, cubes))
@@ -356,6 +368,12 @@
 
         lax.fori_loop(0, cube, finish, 0, unroll=2)
 
+    wait_tiles(l_in, snd.at[INC], 0, cubes * (cube - 1) // 2)
+
+    @pl.when(owner)
+    def _():
+        wait_tiles(lz_in, snd.at[R], 1, tiles - 1)
+
     for i in range(2):
         mine = 2 * d + i == tile
 
@@ -367,28 +385,6 @@
         @pl.when(mine)
         def _(i=i):
             rgrad_ref[:, i * 128:(i + 1) * 128] = r_out[0]
-
-    drains = ((S, s1), (W, w1), (LP, l_in), (A, a_in), (B, b_in), (E, e_in))
-    for kind, buf in drains:
-        wait_tiles(buf, snd.at[kind], 1, buf.shape[0] - 1)
-    wait_tiles(l_in, snd.at[INC], 0, cubes * (cube - 1) // 2)
-
-    @pl.when(h == 1)
-    def _():
-        wait_tiles(f_in, snd.at[TW], 0, cubes)
-
-    for i in range(2):
-        @pl.when(home(2 * d + i) != z)
-        def _():
-            wait_tiles(lsum, snd.at[LZ], 0, 1)
-    for half in range(2):
-        @pl.when(to_p + half != p)
-        def _():
-            wait_tiles(x_out, snd.at[X], 0, 1)
-
-    @pl.when(owner)
-    def _():
-        wait_tiles(lz_in, snd.at[R], 1, tiles - 1)
 
 
 def write_out(gin, rgrad, gin_hbm, rgrad_hbm, sem):
@@ -457,7 +453,7 @@
         out_shape=shapes,
         in_specs=[in_vmem, in_vmem],
         out_specs=(anywhere, anywhere),
-        scratch_shapes=[pltpu.SemaphoreType.DMA((9,))],
+        scratch_shapes=[pltpu.SemaphoreType.DMA((3,))],
         compiler_params=pltpu.CompilerParams(vmem_limit_bytes=1 << 20),
         name="write_out",
     )(*kept)

time: 63.8 us -> 63.7 us (level)
  no operation moved by 1% of the time
where the time goes in v6:
time: 63.7 us; the launch traced here: 63.5 us
  Pallas kernels  62.9 us (99%)
  between operations  0.64 us (1%)
    pallas_call x1, Pallas kernels, local(): pl.pallas_call(functools.partial(kernel, tiles, cube), out_shape=tuple((v...  61.9 us

profile of v6, /device:TPU:3, one launch (start us, length us, event | category | flops | bytes accessed | tf_op | source)
XLA Modules:
  0.0 63.5 jit_solution(7096192924027892023)
XLA Ops:
  0.6 61.9 %modal_backward.1 = (bf16[1,128,4096]{2,1,0:T(8,128)(2,1)S(1)}, f32[8,256]{1,0:T(8,128)S(1)}) custom-call(f32[8]{0:T(128)} %rates.1, bf16[1,128,4096]{2,1,0:T(8,128)(2,1)} %g_hbm.1, bf16[1,128,4096]{2,1,0:T(8,128)(2,1)} %x_hbm.1, f32[8,4096]{1,0:T(8,128)} %res_hbm.1), custom_call_target="tpu_custom_call" | custom-call | tf_op jit(solution)/shard_map/modal_backward/pallas_call | solution.py:421
  62.6 1.0 %write_out.1 = (bf16[1,128,4096]{2,1,0:T(8,128)(2,1)}, f32[8,256]{1,0:T(8,128)}) custom-call(bf16[1,128,4096]{2,1,0:T(8,128)(2,1)S(1)} %get-tuple-element.4.gin, f32[8,256]{1,0:T(8,128)S(1)} %get-tuple-element.5.rgrad), custom_call_target="tpu_custom_call" | custom-call | tf_op jit(solution)/shard_map/write_out/pallas_call | solution.py:451

commit v7 on v6

--- a/solution.py
+++ b/solution.py
@@ -116,6 +116,7 @@
         dst[0] = src[pl.ds(q * cubes, cubes)]
 
     level_1(S, s_out, s1)
+    level_1(W, w_out, w1)
 
     lag = (
         lax.broadcasted_iota(jnp.int32, (rows, rows), 1)
@@ -146,9 +147,7 @@
             l_out[2 * i + t] = lp[:, t * 128:(t + 1) * 128]
         return c
 
-    lax.fori_loop(0, tiles // 4, local, 0)
-    level_1(W, w_out, w1)
-    lax.fori_loop(tiles // 4, tiles // 2, local, 0)
+    lax.fori_loop(0, tiles // 2, local, 0)
 
     got(S, s1)
     f = jnp.zeros((cubes, modes, 128), F32)
@@ -177,6 +176,17 @@
         wj = w1[wrap(j - q, cube)]
         weight = wj + decay[None] * weight
         cross = cross + intra[j] * wj
+    mine = pl.ds(q * cubes, cubes)
+    l_out[mine] = l_out[mine] + cross
+
+    def send_l(j, c):
+        to = wrap(p + j)
+        pair = pl.ds(2 * lax.div(to, 2), 2)
+        send(LP, l_out.at[pair], l_in.at[tiles - j], plane(to))
+        return c
+
+    lax.fori_loop(1, tiles, send_l, 0)
+
     b_out[...] = weight
 
     def far_first(i):
@@ -191,17 +201,6 @@
 
     lax.fori_loop(1, cubes, send_b, 0)
     b_in[0] = b_out[place(e)]
-
-    mine = pl.ds(q * cubes, cubes)
-    l_out[mine] = l_out[mine] + cross
-
-    def send_l(j, c):
-        to = wrap(p + j)
-        pair = pl.ds(2 * lax.div(to, 2), 2)
-        send(LP, l_out.at[pair], l_in.at[tiles - j], plane(to))
-        return c
-
-    lax.fori_loop(1, tiles, send_l, 0)
 
     got(LP, l_in)
     lsum[...] = l_out[pl.ds(2 * d, 2)] + jnp.sum(l_in[1:tiles], axis=0)

time: 63.7 us -> 63.7 us (level)
  no operation moved by 1% of the time
where the time goes in v7:
time: 63.7 us; the launch traced here: 63.6 us
  Pallas kernels  62.9 us (99%)
  between operations  0.64 us (1%)
    pallas_call x1, Pallas kernels, local(): pl.pallas_call(functools.partial(kernel, tiles, cube), out_shape=tuple((v...  61.9 us

profile of v7, /device:TPU:3, one launch (start us, length us, event | category | flops | bytes accessed | tf_op | source)
XLA Modules:
  0.0 63.6 jit_solution(11095498243520302008)
XLA Ops:
  0.6 61.9 %modal_backward.1 = (bf16[1,128,4096]{2,1,0:T(8,128)(2,1)S(1)}, f32[8,256]{1,0:T(8,128)S(1)}) custom-call(f32[8]{0:T(128)} %rates.1, bf16[1,128,4096]{2,1,0:T(8,128)(2,1)} %g_hbm.1, bf16[1,128,4096]{2,1,0:T(8,128)(2,1)} %x_hbm.1, f32[8,4096]{1,0:T(8,128)} %res_hbm.1), custom_call_target="tpu_custom_call" | custom-call | tf_op jit(solution)/shard_map/modal_backward/pallas_call | solution.py:420
  62.6 1.0 %write_out.1 = (bf16[1,128,4096]{2,1,0:T(8,128)(2,1)}, f32[8,256]{1,0:T(8,128)}) custom-call(bf16[1,128,4096]{2,1,0:T(8,128)(2,1)S(1)} %get-tuple-element.4.gin, f32[8,256]{1,0:T(8,128)S(1)} %get-tuple-element.5.rgrad), custom_call_target="tpu_custom_call" | custom-call | tf_op jit(solution)/shard_map/write_out/pallas_call | solution.py:450
